TPU v7x, 512 devices: a whole 4x8x8 slice. The times are simulated.
512 devices in a mesh: dp: 32 (over y, x), expert: 16 (over z, core).
Axes of the slice: x: 4, y: 8, z: 8, core: 2. Of those that a mesh axis runs over, the one named last changes fastest.
Arguments:
- features: bfloat16 [16384, 1536], P(('dp', 'expert')), may hold values from -6 to 6
- classes: int32 [16384], P(('dp', 'expert')), may hold values from 0 to 15, as said below
- live_counts: int32 [512], P(('dp', 'expert')), may hold values from 2 to 32, as said below
- cotangent: bfloat16 [16384, 1536], P(('dp', 'expert')), may hold values from -0.75 to 0.75
- up_weight: bfloat16 [16, 6144, 1536], P('expert', 'dp'), may hold values from -0.15625 to 0.15625
- down_weight: bfloat16 [16, 6144, 1536], P('expert', 'dp'), may hold values from -0.078125 to 0.078125
Outputs:
- mixed: bfloat16 [16384, 1536], P(('dp', 'expert'))
- up_grad: float32 [16, 6144, 1536], P('expert', 'dp')
- down_grad: float32 [16, 6144, 1536], P('expert', 'dp')
Inputs may be any that keep to these rules, and one draw needn't show every extreme that they name: `classes`: each device's 32 slots name every class exactly 2 times, and slots 0 to 1 of every device name one common class. `live_counts`: entry i counts the live slots of device i, which are its first ones; some device has all 32 live.
All inputs are finite; a program needn't handle non-finite values.
Results may differ from a plain program's by a relative error of at most 0.02.
Values may be sent and summed in bfloat16 or wider, within the bound.
A program may use at most 64 MiB of HBM per device.

v0:
```python
from functools import partial

import jax
import jax.numpy as jnp
from jax import lax
from jax.sharding import PartitionSpec as P


def slot_table(group_classes, group_counts, span, expert_count):
    groups, row_count = group_classes.shape
    position = lax.broadcasted_iota(jnp.int32, (groups, row_count), 1)
    live = position < group_counts[:, None]
    labels = lax.broadcasted_iota(jnp.int32, (1, 1, expert_count), 2)
    member = ((group_classes[:, :, None] == labels) & live[:, :, None]).astype(jnp.float32)
    later = lax.broadcasted_iota(jnp.int32, (row_count, row_count), 0)
    sooner = lax.broadcasted_iota(jnp.int32, (row_count, row_count), 1)
    earlier = (sooner < later).astype(jnp.float32)
    before = jnp.einsum("rs,gse->gre", earlier, member)
    place = jnp.sum(before * member, axis=2).astype(jnp.int32)
    target = group_classes * span + place
    slots = lax.broadcasted_iota(jnp.int32, (1, expert_count * span, 1), 1)
    chosen = (target[:, None, :] == slots) & live[:, None, :]
    return chosen.astype(jnp.bfloat16)


def local(features, classes, live_counts, cotangent, up_weight, down_weight):
    expert_count = lax.axis_size("expert") * up_weight.shape[0]
    row_count, width = features.shape
    span = row_count // expert_count
    block = expert_count * span
    up_local = up_weight[0]
    down_local = down_weight[0]
    own_table = slot_table(classes[None, :], live_counts, span, expert_count)[0]

    def spread(stacked):
        layers = stacked.shape[0]
        sent = jnp.einsum("tr,krd->ktd", own_table, stacked, preferred_element_type=jnp.float32)
        sent = sent.astype(jnp.bfloat16).reshape(layers, expert_count, span, width)
        arrived = lax.all_to_all(sent, "expert", split_axis=1, concat_axis=1, tiled=True)
        flat = arrived.reshape(layers, block, width)
        return lax.all_gather(flat, "dp", axis=1, tiled=True)

    rows_in = spread(features[None])[0]
    grads_in = None
    inner = jnp.dot(rows_in, up_local.T, preferred_element_type=jnp.float32)
    hidden = jax.nn.gelu(inner, approximate=True).astype(jnp.bfloat16)
    mine = lax.psum_scatter(
        jnp.dot(hidden, down_local, preferred_element_type=jnp.float32).astype(jnp.bfloat16),
        "dp",
        scatter_dimension=0,
        tiled=True,
    )
    going_back = mine.reshape(expert_count, span, width)
    returned = lax.all_to_all(going_back, "expert", split_axis=0, concat_axis=0, tiled=True)
    mixed = jnp.dot(
        own_table.T, returned.reshape(block, width), preferred_element_type=jnp.float32
    ).astype(jnp.bfloat16)
    grads_in = spread(cotangent[None])[0]
    slope = jnp.dot(grads_in, down_local.T, preferred_element_type=jnp.float32)
    _, pull = jax.vjp(partial(jax.nn.gelu, approximate=True), inner)
    inner_grad = pull(slope)[0].astype(jnp.bfloat16)
    grad_down = jnp.dot(hidden.T, grads_in, preferred_element_type=jnp.float32)
    grad_up = jnp.dot(inner_grad.T, rows_in, preferred_element_type=jnp.float32)
    return (mixed, grad_up[None], grad_down[None])


def solution(mesh):
    placed = (
        P(("dp", "expert"), None),
        P(("dp", "expert")),
        P(("dp", "expert")),
        P(("dp", "expert"), None),
        P("expert", "dp", None),
        P("expert", "dp", None),
    )
    return jax.shard_map(
        local,
        mesh=mesh,
        in_specs=placed,
        out_specs=(P(("dp", "expert"), None), P("expert", "dp", None), P("expert", "dp", None)),
        check_vma=False,
    )
```

profile of v0, /device:TPU:1, one launch (start us, length us, event | category | flops | bytes accessed | tf_op | source)
XLA Modules:
  0.0 452.1 jit_solution(10627285349762428786)
XLA Ops:
  7.2 0.0 copy-start
  7.2 0.0 all-gather.3.cloned.1.call-start
  7.9 1.0 fusion.17
  8.9 0.7 convert_add_fusion
  9.6 1.0 fusion.14
  10.7 20.1 %all_to_all.15 = bf16[1,16,2,1536]{3,2,0,1:T(2,128)(2,1)S(1)} all-to-all(bf16[1,16,2,1536]{3,2,0,1:T(2,128)(2,1)S(1)} %bitcast.62), channel_id=1, replica_groups=mesh['dp'=32,'expert'=16] {'expert'}, dimensions={1} | all-to-all | bytes 196608 | tf_op jit(solution)/shard_map/all_to_all | solution.py:39
  30.7 0.7 reshape.157
  31.4 0.0 all-gather.3.cloned.1.call-update
  31.5 0.0 all-gather.5.cloned.1.call-start
  31.5 1.0 fusion.15
  32.6 10.9 %all_to_all.16 = bf16[1,16,2,1536]{3,2,0,1:T(2,128)(2,1)S(1)} all-to-all(bf16[1,16,2,1536]{3,2,0,1:T(2,128)(2,1)S(1)} %bitcast.63), channel_id=1, replica_groups=mesh['dp'=32,'expert'=16] {'expert'}, dimensions={1} | all-to-all | bytes 196608 | tf_op jit(solution)/shard_map/all_to_all | solution.py:39
  43.5 0.7 reshape.161
  44.1 0.0 all-gather.5.cloned.1.call-update
  44.2 0.0 reduce-scatter.2.cloned.1.call-start
  44.2 64.5 %all-gather.3.cloned.1.call-done = bf16[1,1024,1536]{2,1,0:T(8,128)(2,1)} async-done(((bf16[1,32,1536]{2,1,0:T(8,128)(2,1)}), bf16[1,1024,1536]{2,1,0:T(8,128)(2,1)}) %all-gather.3.cloned.1.call-update) | async-done | bytes 3145744 | tf_op jit(solution)/shard_map/all_gather | solution.py:41
  108.7 3.2 fusion.6
  111.9 0.0 copy-done
  111.9 2.8 convolution_convert_fusion
  114.7 0.0 reduce-scatter.2.cloned.1.call-update
  114.7 79.6 %all-gather.5.cloned.1.call-done = bf16[1,1024,1536]{2,1,0:T(8,128)(2,1)} async-done(((bf16[1,32,1536]{2,1,0:T(8,128)(2,1)}), bf16[1,1024,1536]{2,1,0:T(8,128)(2,1)}) %all-gather.5.cloned.1.call-update) | async-done | bytes 3145744 | tf_op jit(solution)/shard_map/all_gather | solution.py:41
  194.3 5.9 %fusion.8 = f32[1,192,1536]{2,1,0:T(8,128)} fusion(bf16[1,1024,1536]{2,1,0:T(8,128)(2,1)} %all-gather.3.cloned.1.call-done, f32[1024,192]{0,1:T(8,128)S(1)} %fusion.6, bf16[1,1024,1536]{2,1,0:T(8,128)(2,1)} %all-gather.5.cloned.1.call-done, bf16[1,192,1536]{2,1,0:T(8,128)(2,1)S(1)} %copy-done), kind=kOutput, calls=%fused_computation.9 | convolution fusion | flops 1211891712 | bytes 8847360 | tf_op jit(solution)/shard_map/dot_general | solution.py:63
  200.2 221.3 %reduce-scatter.2.cloned.1.call-done = bf16[32,1536]{1,0:T(8,128)(2,1)} async-done(((bf16[1024,1536]{1,0:T(8,128)(2,1)}), bf16[32,1536]{1,0:T(8,128)(2,1)}) %reduce-scatter.2.cloned.1.call-update) | async-done | bytes 98320 | tf_op jit(solution)/shard_map/reduce_scatter | solution.py:47
  421.5 1.6 reshape.158
  423.1 13.1 %all-to-all-start.1 = ((bf16[16,2,1536]{2,1,0:T(2,128)(2,1)}), bf16[16,2,1536]{2,1,0:T(2,128)(2,1)S(1)}, u32[]{:S(2)}, u32[]{:S(2)}) async-start(bf16[16,2,1536]{2,1,0:T(2,128)(2,1)} %reshape.158), calls=%async_computation.2 | async-start | bytes 196608 | tf_op jit(solution)/shard_map/all_to_all | solution.py:54
  436.2 3.7 fusion.11
  439.9 4.7 %all-to-all-done.1 = bf16[16,2,1536]{2,1,0:T(2,128)(2,1)S(1)} async-done(((bf16[16,2,1536]{2,1,0:T(2,128)(2,1)}), bf16[16,2,1536]{2,1,0:T(2,128)(2,1)S(1)}, u32[]{:S(2)}, u32[]{:S(2)}) %all-to-all-start.1) | async-done | bytes 98336 | tf_op jit(solution)/shard_map/all_to_all | solution.py:54
  444.7 0.9 convolution_convert_fusion.2
  (4 shorter events, 0.1 us)
Async XLA Ops:
  7.2 104.7 %copy-start = (bf16[1,192,1536]{2,1,0:T(8,128)(2,1)S(1)}, bf16[1,192,1536]{2,1,0:T(8,128)(2,1)}, u32[]{:S(2)}) copy-start(bf16[1,192,1536]{2,1,0:T(8,128)(2,1)} %param.11) | copy-start | bytes 1769476
  7.2 101.5 %all-gather.3.cloned.1.call-start = ((), (), s32[]{:S(2)}) async-start(), calls=%async_computation.4 | async-start | bytes 3244032 | tf_op jit(solution)/shard_map/all_gather | solution.py:41
  31.5 162.8 %all-gather.5.cloned.1.call-start = ((), (), s32[]{:S(2)}) async-start(), calls=%async_computation.6 | async-start | bytes 3244032 | tf_op jit(solution)/shard_map/all_gather | solution.py:41
  44.2 377.3 %reduce-scatter.2.cloned.1.call-start = ((), (), s32[]{:S(2)}) async-start(), calls=%async_computation.5 | async-start | bytes 3244032 | tf_op jit(solution)/shard_map/reduce_scatter | solution.py:47
  423.1 21.6 %all-to-all-start.1 = ((bf16[16,2,1536]{2,1,0:T(2,128)(2,1)}), bf16[16,2,1536]{2,1,0:T(2,128)(2,1)S(1)}, u32[]{:S(2)}, u32[]{:S(2)}) async-start(bf16[16,2,1536]{2,1,0:T(2,128)(2,1)} %reshape.158), calls=%async_computation.2 | async-start | bytes 196608 | tf_op jit(solution)/shard_map/all_to_all | solution.py:54
Sparse Core Ops, SparseCore 0:
  31.6 77.0 all-gather.2
  112.5 81.7 all-gather.4
  198.7 222.7 reduce-scatter.1
where the time goes:
time: 452 us
  waiting for transfers between devices  370 us (82%)
  blocking collectives  30.9 us (7%)
  matrix products  19.5 us (4%)
  between operations  14.5 us (3%)
  starting transfers between devices  13.2 us (3%)
    reduce_scatter x1, waiting for transfers between devices, local(): lax.psum_scatter(jnp.dot(hidden, down_local, preferred_element_type=jnp.f...  221 us
    all_gather x2, waiting for transfers between devices, spread(): return lax.all_gather(flat, 'dp', axis=1, tiled=True)  144 us
    all_to_all x2, blocking collectives, spread(): lax.all_to_all(sent, 'expert', split_axis=1, concat_axis=1, tiled=True)  30.9 us
    all_to_all x1, starting transfers between devices, local(): lax.all_to_all(going_back, 'expert', split_axis=0, concat_axis=0, tiled=T...  13.1 us
  transfers between devices with their start and end apart: 4, of which 4 were waited for; matrix products, arithmetic and copies ran while one was open for 4% of the time, Pallas kernels for 0%

commit v1 on v0

v1 whole, which is shorter than its diff:
```python
import functools

import jax
import jax.numpy as jnp
from jax import lax
from jax.experimental import pallas as pl
from jax.experimental.pallas import tpu as pltpu
from jax.sharding import PartitionSpec as P

NY, NX = 8, 4
MESH = pl.DeviceIdType.MESH
SEMS = 52
ROOT = 0.7978845608028654
CUBE = 0.044715


def slot_table(group_classes, group_counts, span, expert_count):
    row_count = group_classes.shape[0]
    position = lax.broadcasted_iota(jnp.int32, (1, row_count), 1)
    live = position < group_counts
    same = group_classes[:, None] == group_classes[None, :]
    later = lax.broadcasted_iota(jnp.int32, (row_count, row_count), 0)
    sooner = lax.broadcasted_iota(jnp.int32, (row_count, row_count), 1)
    place = jnp.sum((same & (sooner < later)).astype(jnp.int32), axis=1)
    target = group_classes * span + place
    slots = lax.broadcasted_iota(jnp.int32, (expert_count * span, 1), 0)
    chosen = (target[None, :] == slots) & live
    return chosen.astype(jnp.bfloat16)


class Line:
    def __init__(self, count, here, view, right, left, sems, take, sent):
        self.count, self.here, self.view = count, here, view
        self.right, self.left = right, left
        self.send_sem, self.recv_sem = sems
        self.base = take(count)
        self.sent = sent

    def at(self, offset):
        return lax.rem(self.here + offset + self.count, self.count)

    def rows(self, half, way):
        rows = 32
        if not half:
            return pl.ds(0, rows)
        return pl.ds(0, rows // 2) if way == 0 else pl.ds(rows // 2, rows // 2)

    def copy(self, step, way, src, dst):
        k = self.base + 2 * (step - 1) + way
        return pltpu.make_async_remote_copy(
            src_ref=src,
            dst_ref=dst,
            send_sem=self.send_sem.at[k],
            recv_sem=self.recv_sem.at[k],
            device_id=self.right if way == 0 else self.left,
            device_id_type=MESH,
        )


class Spread(Line):
    def start(self, step):
        for way, sign in ((0, -1), (1, 1)):
            ref = self.view(self.at(sign * (step - 1)), self.rows(step == self.count // 2, way))
            copy = self.copy(step, way, ref, ref)
            copy.start()
            self.sent.append(copy)

    def wait(self, step):
        for way, sign in ((0, -1), (1, 1)):
            ref = self.view(self.at(sign * step), self.rows(step == self.count // 2, way))
            self.copy(step, way, ref, ref).wait_recv()


class Gather(Line):
    def __init__(self, *args, slot):
        super().__init__(*args)
        self.slot = slot

    def start(self, step):
        for way, sign in ((0, 1), (1, -1)):
            rows = self.rows(step == 1, way)
            src = self.view(self.at(sign * (self.count // 2 + 1 - step)), rows)
            copy = self.copy(step, way, src, self.slot(way, step - 1, rows))
            copy.start()
            self.sent.append(copy)

    def add(self, step):
        for way, sign in ((0, 1), (1, -1)):
            rows = self.rows(step == 1, way)
            here = self.view(self.at(sign * (self.count // 2 - step)), rows)
            came = self.slot(way, step - 1, rows)
            self.copy(step, way, came, came).wait_recv()
            here[...] = (here[...].astype(jnp.float32) + came[...].astype(jnp.float32)).astype(
                here.dtype
            )


def counter():
    state = [0]

    def take(count):
        base = state[0]
        state[0] += count
        return base

    return take


def block_kernel(
    cut, x_ref, g_ref, up_ref, down_ref, mine_ref, gup_ref, gdown_ref,
    xs, gs, part, ra2, ra1, rb2, rb1, slope_of, hid, igr,
    own_sem, xsend, xrecv, gsend, grecv, rsend, rrecv,
):
    me = lax.axis_index("dp")
    e = lax.axis_index("expert")
    y, x = lax.div(me, NX), lax.rem(me, NX)
    width = x_ref.shape[1]
    lo, hi = pl.ds(0, cut), pl.ds(cut, width - cut)

    def device(yy, xx):
        return (lax.rem(yy + NY, NY) * NX + lax.rem(xx + NX, NX), e)

    xr, xl = device(y, x + 1), device(y, x - 1)
    yr, yl = device(y + 1, x), device(y - 1, x)

    barrier = pltpu.get_barrier_semaphore()
    for peer in (xr, xl, yr, yl):
        pl.semaphore_signal(barrier, inc=1, device_id=peer, device_id_type=MESH)
    pl.semaphore_wait(barrier, 4)

    owns = [
        pltpu.make_async_copy(x_ref, xs.at[y, x], own_sem.at[0]),
        pltpu.make_async_copy(g_ref, gs.at[y, x], own_sem.at[1]),
    ]
    for own in owns:
        own.start()
    for own in owns:
        own.wait()

    sent = []
    offsets = (0, 1, -1, 2, -2, 3, -3, 4)

    def row_of(offset):
        return lax.rem(y + offset + NY, NY)

    def gather_rounds(t, send_sem, recv_sem):
        take, sems = counter(), (send_sem, recv_sem)
        a1 = Spread(NX, x, lambda i, r: t.at[y, i, r, lo], xr, xl, sems, take, sent)
        a2 = Spread(NY, y, lambda i, r: t.at[i, :, r, lo], yr, yl, sems, take, sent)
        b1 = Spread(NY, y, lambda i, r: t.at[i, x, r, hi], yr, yl, sems, take, sent)
        b2 = {
            o: Spread(
                NX, x, (lambda yy: lambda i, r: t.at[yy, i, r, hi])(row_of(o)),
                xr, xl, sems, take, sent,
            )
            for o in offsets
        }

        def turn(*offs):
            for o in offs:
                b2[o].wait(1)
                b2[o].start(2)

        a1.start(1)
        b1.start(1)
        b2[0].start(1)
        yield
        b1.wait(1)
        b1.start(2)
        a1.wait(1)
        a1.start(2)
        b2[1].start(1)
        b2[-1].start(1)
        yield
        b1.wait(2)
        b1.start(3)
        a1.wait(2)
        a2.start(1)
        b2[2].start(1)
        b2[-2].start(1)
        turn(0)
        yield
        b1.wait(3)
        b1.start(4)
        b2[3].start(1)
        b2[-3].start(1)
        turn(1, -1)
        yield
        b1.wait(4)
        b2[4].start(1)
        a2.wait(1)
        a2.start(2)
        turn(2, -2)
        yield
        a2.wait(2)
        a2.start(3)
        turn(3, -3)
        yield
        a2.wait(3)
        a2.start(4)
        turn(4)
        yield
        for o in offsets:
            b2[o].wait(2)
        a2.wait(4)

    def sum_rounds():
        take, sems = counter(), (rsend, rrecv)
        a2 = Gather(
            NY, y, lambda i, r: part.at[i, :, r, lo], yr, yl, sems, take, sent,
            slot=lambda w, s, r: ra2.at[w, s, :, r, :],
        )
        a1 = Gather(
            NX, x, lambda i, r: part.at[y, i, r, lo], xr, xl, sems, take, sent,
            slot=lambda w, s, r: ra1.at[w, s, r, :],
        )
        b1 = Gather(
            NY, y, lambda i, r: part.at[i, x, r, hi], yr, yl, sems, take, sent,
            slot=lambda w, s, r: rb1.at[w, s, r, :],
        )
        b2 = {
            o: Gather(
                NX, x, (lambda yy: lambda i, r: part.at[yy, i, r, hi])(row_of(o)),
                xr, xl, sems, take, sent,
                slot=(lambda n: lambda w, s, r: rb2.at[n, w, s, r, :])(n),
            )
            for n, o in enumerate(offsets)
        }

        def turn(*offs):
            for o in offs:
                b2[o].add(1)
                b2[o].start(2)

        def done(*offs):
            for o in offs:
                b2[o].add(2)

        a2.start(1)
        for o in (4, 3, -3, 2, -2):
            b2[o].start(1)
        yield
        turn(4)
        a2.add(1)
        a2.start(2)
        turn(3, -3)
        for o in (1, -1, 0):
            b2[o].start(1)
        yield
        done(4)
        b1.start(1)
        turn(2, -2)
        yield
        a2.add(2)
        a2.start(3)
        done(3, -3)
        b1.add(1)
        b1.start(2)
        turn(1, -1, 0)
        yield
        a2.add(3)
        a2.start(4)
        done(2, -2)
        b1.add(2)
        b1.start(3)
        yield
        a2.add(4)
        a1.start(1)
        done(1, -1)
        b1.add(3)
        b1.start(4)
        yield
        a1.add(1)
        a1.start(2)
        done(0)
        yield
        b1.add(4)
        a1.add(2)

    nt = (((1,), (1,)), ((), ()))
    tn = (((0,), (0,)), ((), ()))
    chunk = NX * 32

    def forward(first, last):
        def body(c, carry):
            rows = xs[c].reshape(chunk, width)
            v = lax.dot_general(up_ref[...], rows, nt, preferred_element_type=jnp.float32)
            t = jnp.tanh(ROOT * (v + CUBE * v * v * v))
            columns = pl.ds(pl.multiple_of(c * chunk, chunk), chunk)
            slope_of[:, columns] = 0.5 * (1.0 + t) + 0.5 * v * (1.0 - t * t) * (
                ROOT * (1.0 + 3.0 * CUBE * v * v)
            )
            h = (0.5 * v * (1.0 + t)).astype(jnp.bfloat16)
            hid[:, columns] = h
            p = lax.dot_general(h, down_ref[...], tn, preferred_element_type=jnp.float32)
            part[c] = p.astype(jnp.bfloat16).reshape(NX, 32, width)
            return carry

        lax.fori_loop(first, last, body, 0)

    def backward():
        def body(c, carry):
            rows = gs[c].reshape(chunk, width)
            v = lax.dot_general(down_ref[...], rows, nt, preferred_element_type=jnp.float32)
            columns = pl.ds(pl.multiple_of(c * chunk, chunk), chunk)
            igr[:, columns] = (v * slope_of[:, columns]).astype(jnp.bfloat16)
            return carry

        lax.fori_loop(0, NY, body, 0)

    def weight_sums(left, t, out):
        tile = min(256, width)

        def body(j, carry):
            columns = pl.ds(pl.multiple_of(j * tile, tile), tile)
            rows = t[:, :, :, columns].reshape(NY * chunk, tile)
            out[:, columns] = jnp.dot(left[...], rows, preferred_element_type=jnp.float32)
            return carry

        lax.fori_loop(0, width // tile, body, 0)

    xg = gather_rounds(xs, xsend, xrecv)
    gg = gather_rounds(gs, gsend, grecv)
    for _ in range(4):
        next(xg)
    next(gg)
    next(xg)
    next(gg)
    next(xg)
    next(gg)
    next(xg)
    next(gg)
    next(xg, None)
    forward(0, NY // 2)
    next(gg)
    forward(NY // 2, NY)
    rg = sum_rounds()
    next(rg)
    next(gg)
    next(rg)
    next(gg)
    next(rg)
    next(gg, None)
    backward()
    next(rg)
    weight_sums(hid, gs, gdown_ref)
    next(rg)
    weight_sums(igr, xs, gup_ref)
    for _ in rg:
        pass
    mine_ref[...] = part[y, x]
    for copy in sent:
        copy.wait_send()


def block(rows, grads, up, down):
    n, width = rows.shape
    units = up.shape[0]
    cut = max(1, (width // 128) * 5 // 12) * 128
    rest = width - cut
    bf, f32 = jnp.bfloat16, jnp.float32
    vmem = pl.BlockSpec(memory_space=pltpu.VMEM)
    dma = lambda k: pltpu.SemaphoreType.DMA((k,))
    return pl.pallas_call(
        functools.partial(block_kernel, cut),
        out_shape=(
            jax.ShapeDtypeStruct((n, width), bf),
            jax.ShapeDtypeStruct((units, width), f32),
            jax.ShapeDtypeStruct((units, width), f32),
        ),
        in_specs=[vmem] * 4,
        out_specs=(vmem,) * 3,
        scratch_shapes=[
            pltpu.VMEM((NY, NX, n, width), bf),
            pltpu.VMEM((NY, NX, n, width), bf),
            pltpu.VMEM((NY, NX, n, width), bf),
            pltpu.VMEM((2, 4, NX, n, cut), bf),
            pltpu.VMEM((2, 2, n, cut), bf),
            pltpu.VMEM((8, 2, 2, n, rest), bf),
            pltpu.VMEM((2, 4, n, rest), bf),
            pltpu.VMEM((units, NY * NX * n), f32),
            pltpu.VMEM((units, NY * NX * n), bf),
            pltpu.VMEM((units, NY * NX * n), bf),
            dma(2),
        ]
        + [dma(SEMS)] * 6,
        compiler_params=pltpu.CompilerParams(
            collective_id=0, has_side_effects=True, vmem_limit_bytes=58 * 1024 * 1024
        ),
    )(rows, grads, up, down)


def local(features, classes, live_counts, cotangent, up_weight, down_weight):
    expert_count = lax.axis_size("expert")
    row_count, width = features.shape
    span = row_count // expert_count
    own_table = slot_table(classes, live_counts[0], span, expert_count)
    both = jnp.concatenate([features, cotangent], axis=1)
    send = jnp.dot(own_table, both, preferred_element_type=jnp.float32).astype(jnp.bfloat16)
    send = send.reshape(expert_count, span, 2 * width)
    came = lax.all_to_all(send, "expert", split_axis=0, concat_axis=0, tiled=True)
    came = came.reshape(row_count, 2 * width)
    mine, grad_up, grad_down = block(
        came[:, :width], came[:, width:], up_weight[0], down_weight[0]
    )
    back = mine.reshape(expert_count, span, width)
    back = lax.all_to_all(back, "expert", split_axis=0, concat_axis=0, tiled=True)
    mixed = jnp.dot(
        own_table.T, back.reshape(row_count, width), preferred_element_type=jnp.float32
    ).astype(jnp.bfloat16)
    return (mixed, grad_up[None], grad_down[None])


def solution(mesh):
    placed = (
        P(("dp", "expert"), None),
        P(("dp", "expert")),
        P(("dp", "expert")),
        P(("dp", "expert"), None),
        P("expert", "dp", None),
        P("expert", "dp", None),
    )
    return jax.shard_map(
        local,
        mesh=mesh,
        in_specs=placed,
        out_specs=(P(("dp", "expert"), None), P("expert", "dp", None), P("expert", "dp", None)),
        check_vma=False,
    )
```

time: 452 us -> 129 us (0.29)
  waiting for transfers between devices: 370 us -> 8.49 us
  Pallas kernels: 0 us -> 77.2 us
  matrix products: 19.5 us -> 1.99 us
  between operations: 14.5 us -> 1.32 us
  blocking collectives: 30.9 us -> 21.8 us
    reduce_scatter x1 -> x0, waiting for transfers between devices: 221 us -> none  [local(): lax.psum_scatter(jnp.dot(hidden, down_local, preferred_element_type=jnp.f...]
    all_gather x2 -> x0, waiting for transfers between devices: 144 us -> none  [spread(): return lax.all_gather(flat, 'dp', axis=1, tiled=True)]
    pallas_call x0 -> x1, Pallas kernels: none -> 77.2 us  [block(): pl.pallas_call(functools.partial(block_kernel, cut), out_shape=(jax.Shape...]
    dot_general x8 -> x2, matrix products: 19.5 us -> 1.99 us  [the longest x1 1.12 us: local(): jnp.dot(own_table, both, preferred_element_type=jnp.float32)]
    all_to_all x2 -> x1, blocking collectives: 30.9 us -> 21.8 us  [local(): lax.all_to_all(send, 'expert', split_axis=0, concat_axis=0, tiled=True)]
  transfers between devices with their start and end apart: 4 -> 1, of which waited for: 4 -> 1; matrix products, arithmetic and copies ran while one was open for 4% -> 0% of each run, Pallas kernels for 0% -> 0%
where the time goes in v1:
time: 129 us
  Pallas kernels  77.2 us (60%)
  blocking collectives  21.8 us (17%)
  starting transfers between devices  10.6 us (8%)
  waiting for transfers between devices  8.49 us (7%)
  local copies, waits for them, and re-layouts  5.92 us (5%)
  matrix products  1.99 us (2%)
  other arithmetic  1.58 us (1%)
  between operations  1.32 us (1%)
    pallas_call x1, Pallas kernels, block(): pl.pallas_call(functools.partial(block_kernel, cut), out_shape=(jax.Shape...  77.2 us
    all_to_all x1, blocking collectives, local(): lax.all_to_all(send, 'expert', split_axis=0, concat_axis=0, tiled=True)  21.8 us
    all_to_all x1, starting transfers between devices, local(): lax.all_to_all(back, 'expert', split_axis=0, concat_axis=0, tiled=True)  10.6 us
    all_to_all x1, waiting for transfers between devices, local(): lax.all_to_all(back, 'expert', split_axis=0, concat_axis=0, tiled=True)  8.49 us
    unnamed x4, local copies, waits for them, and re-layouts  3.47 us
  transfers between devices with their start and end apart: 1, of which 1 were waited for; matrix products, arithmetic and copies ran while one was open for 0% of the time, Pallas kernels for 0%

profile of v1, /device:TPU:1, one launch (start us, length us, event | category | flops | bytes accessed | tf_op | source)
XLA Modules:
  0.0 129.0 jit_solution(4989101800276820234)
XLA Ops:
  1.3 0.9 convert_reduce_fusion
  2.2 0.7 multiply_add_fusion
  2.9 1.1 convolution_convert_fusion
  4.0 0.1 reshape.26
  4.1 21.8 %all_to_all.10 = bf16[16,2,3072]{2,1,0:T(2,128)(2,1)S(1)} all-to-all(bf16[16,2,3072]{2,1,0:T(2,128)(2,1)S(1)} %reshape.26), channel_id=1, replica_groups=mesh['dp'=32,'expert'=16] {'expert'}, dimensions={0} | all-to-all | bytes 393216 | tf_op jit(solution)/shard_map/all_to_all | solution.py:401
  25.9 0.1 reshape.27
  26.0 0.7 fusion.12
  26.7 77.2 %shard_map.85 = (bf16[32,1536]{1,0:T(8,128)(2,1)}, f32[192,1536]{1,0:T(8,128)}, f32[192,1536]{1,0:T(8,128)}) custom-call(bf16[32,1536]{1,0:T(8,128)(2,1)} %get-tuple-element.10.x_ref, bf16[32,1536]{1,0:T(8,128)(2,1)} %get-tuple-element.9.g_ref, bf16[192,1536]{1,0:T(8,128)(2,1)} %bitcast.9, bf16[192,1536]{1,0:T(8,128)(2,1)} %bitcast.10), custom_call_target="tpu_custom_call" | custom-call | tf_op jit(solution)/shard_map/pallas_call | solution.py:364
  103.9 1.6 %reshape.28 = bf16[16,2,1536]{2,1,0:T(2,128)(2,1)} reshape(bf16[32,1536]{1,0:T(8,128)(2,1)} %get-tuple-element.6) | data formatting | bytes 196608 | tf_op jit(solution)/shard_map/reshape | solution.py:406
  105.5 10.6 %all-to-all-start.1 = ((bf16[16,2,1536]{2,1,0:T(2,128)(2,1)}), bf16[16,2,1536]{2,1,0:T(2,128)(2,1)S(1)}, u32[]{:S(2)}, u32[]{:S(2)}) async-start(bf16[16,2,1536]{2,1,0:T(2,128)(2,1)} %reshape.28), calls=%async_computation.1 | async-start | bytes 196608 | tf_op jit(solution)/shard_map/all_to_all | solution.py:407
  116.1 8.5 %all-to-all-done.1 = bf16[16,2,1536]{2,1,0:T(2,128)(2,1)S(1)} async-done(((bf16[16,2,1536]{2,1,0:T(2,128)(2,1)}), bf16[16,2,1536]{2,1,0:T(2,128)(2,1)S(1)}, u32[]{:S(2)}, u32[]{:S(2)}) %all-to-all-start.1) | async-done | bytes 98336 | tf_op jit(solution)/shard_map/all_to_all | solution.py:407
  124.7 0.9 convolution_convert_fusion.1
  125.5 0.0 copy-start
  125.5 2.5 %copy.12 = f32[1,192,1536]{2,1,0:T(8,128)} copy(f32[1,192,1536]{2,1,0:T(8,128)} %bitcast.8) | data formatting | bytes 2359296
  128.0 0.0 copy-done
  128.0 1.0 copy.13
  (2 shorter events, 0.0 us)
Async XLA Ops:
  105.5 19.1 %all-to-all-start.1 = ((bf16[16,2,1536]{2,1,0:T(2,128)(2,1)}), bf16[16,2,1536]{2,1,0:T(2,128)(2,1)S(1)}, u32[]{:S(2)}, u32[]{:S(2)}) async-start(bf16[16,2,1536]{2,1,0:T(2,128)(2,1)} %reshape.28), calls=%async_computation.1 | async-start | bytes 196608 | tf_op jit(solution)/shard_map/all_to_all | solution.py:407
  125.5 2.5 %copy-start = (f32[192,1536]{1,0:T(8,128)S(1)}, f32[192,1536]{1,0:T(8,128)}, u32[]{:S(2)}) copy-start(f32[192,1536]{1,0:T(8,128)} %get-tuple-element.8) | copy-start | bytes 3538948

commit v2 on v1

--- a/solution.py
+++ b/solution.py
@@ -10,11 +10,12 @@
 NY, NX = 8, 4
 MESH = pl.DeviceIdType.MESH
 SEMS = 52
+PAD = 8
 ROOT = 0.7978845608028654
 CUBE = 0.044715
 
 
-def slot_table(group_classes, group_counts, span, expert_count):
+def slot_table(group_classes, group_counts, expert_count):
     row_count = group_classes.shape[0]
     position = lax.broadcasted_iota(jnp.int32, (1, row_count), 1)
     live = position < group_counts
@@ -22,8 +23,8 @@
     later = lax.broadcasted_iota(jnp.int32, (row_count, row_count), 0)
     sooner = lax.broadcasted_iota(jnp.int32, (row_count, row_count), 1)
     place = jnp.sum((same & (sooner < later)).astype(jnp.int32), axis=1)
-    target = group_classes * span + place
-    slots = lax.broadcasted_iota(jnp.int32, (expert_count * span, 1), 0)
+    target = group_classes * PAD + place
+    slots = lax.broadcasted_iota(jnp.int32, (expert_count * PAD, 1), 0)
     chosen = (target[None, :] == slots) & live
     return chosen.astype(jnp.bfloat16)
 
@@ -107,9 +108,9 @@
 
 
 def block_kernel(
-    cut, x_ref, g_ref, up_ref, down_ref, mine_ref, gup_ref, gdown_ref,
-    xs, gs, part, ra2, ra1, rb2, rb1, slope_of, hid, igr,
-    own_sem, xsend, xrecv, gsend, grecv, rsend, rrecv,
+    cut, experts, table_ref, x_ref, g_ref, up_ref, down_ref, mixed_ref, gup_ref, gdown_ref,
+    xs, gs, part, ra2, ra1, rb2, rb1, slope_of, hid, igr, out_to, in_from, wide,
+    own_sem, dsend, drecv, xsend, xrecv, gsend, grecv, rsend, rrecv,
 ):
     me = lax.axis_index("dp")
     e = lax.axis_index("expert")
@@ -123,21 +124,65 @@
     xr, xl = device(y, x + 1), device(y, x - 1)
     yr, yl = device(y + 1, x), device(y - 1, x)
 
+    n = x_ref.shape[0]
+    span = n // experts
+
+    def other(offset):
+        return lax.rem(e + offset + experts, experts)
+
     barrier = pltpu.get_barrier_semaphore()
-    for peer in (xr, xl, yr, yl):
+    for peer in [xr, xl, yr, yl] + [(me, other(d)) for d in range(1, experts)]:
         pl.semaphore_signal(barrier, inc=1, device_id=peer, device_id_type=MESH)
-    pl.semaphore_wait(barrier, 4)
-
-    owns = [
-        pltpu.make_async_copy(x_ref, xs.at[y, x], own_sem.at[0]),
-        pltpu.make_async_copy(g_ref, gs.at[y, x], own_sem.at[1]),
-    ]
-    for own in owns:
-        own.start()
-    for own in owns:
-        own.wait()
-
+
+    def exchange(k, d, way):
+        there = other(d * way)
+        return pltpu.make_async_remote_copy(
+            src_ref=out_to.at[k, there],
+            dst_ref=in_from.at[k, e if way == 1 else there],
+            send_sem=dsend.at[k, d],
+            recv_sem=drecv.at[k, d],
+            device_id=(me, there),
+            device_id_type=MESH,
+        )
+
+    def own(k):
+        return pltpu.make_async_copy(out_to.at[k, e], in_from.at[k, e], own_sem.at[k])
+
+    near = [d for h in range(1, experts // 2 + 1) for d in sorted({h, experts - h})]
+
+    def fill(k, table, rows):
+        spread = jnp.dot(table, rows, preferred_element_type=jnp.float32)
+        out_to[k] = spread.reshape(experts, PAD, width)[:, :span, :].astype(jnp.bfloat16)
+
+    def leave(k):
+        own(k).start()
+        for d in near:
+            copy = exchange(k, d, 1)
+            copy.start()
+            sent.append(copy)
+
+    def arrive(k, table):
+        own(k).wait()
+        for d in near:
+            exchange(k, d, -1).wait_recv()
+        wide[:, :span, :] = in_from[k].astype(jnp.float32)
+        flat = wide[...].reshape(experts * PAD, width).astype(jnp.bfloat16)
+        return lax.dot_general(
+            table, flat, (((0,), (0,)), ((), ())), preferred_element_type=jnp.float32
+        ).astype(jnp.bfloat16)
+
+    wide[...] = jnp.zeros_like(wide)
+    slot = lax.broadcasted_iota(jnp.int32, (experts * PAD, n), 0)
+    row = lax.broadcasted_iota(jnp.int32, (experts * PAD, n), 1)
+    dense = (slot == lax.div(row, span) * PAD + lax.rem(row, span)).astype(jnp.bfloat16)
     sent = []
+    fill(0, table_ref[...], x_ref[...])
+    pl.semaphore_wait(barrier, 3 + experts)
+    leave(0)
+    fill(1, table_ref[...], g_ref[...])
+    leave(1)
+    xs[y, x] = arrive(0, dense)
+
     offsets = (0, 1, -1, 2, -2, 3, -3, 4)
 
     def row_of(offset):
@@ -321,7 +366,10 @@
 
     xg = gather_rounds(xs, xsend, xrecv)
     gg = gather_rounds(gs, gsend, grecv)
-    for _ in range(4):
+    for _ in range(2):
+        next(xg)
+    gs[y, x] = arrive(1, dense)
+    for _ in range(2):
         next(xg)
     next(gg)
     next(xg)
@@ -348,12 +396,14 @@
     weight_sums(igr, xs, gup_ref)
     for _ in rg:
         pass
-    mine_ref[...] = part[y, x]
+    fill(2, dense, part[y, x])
+    leave(2)
+    mixed_ref[...] = arrive(2, table_ref[...])
     for copy in sent:
         copy.wait_send()
 
 
-def block(rows, grads, up, down):
+def block(table, rows, grads, up, down, experts):
     n, width = rows.shape
     units = up.shape[0]
     cut = max(1, (width // 128) * 5 // 12) * 128
@@ -362,13 +412,13 @@
     vmem = pl.BlockSpec(memory_space=pltpu.VMEM)
     dma = lambda k: pltpu.SemaphoreType.DMA((k,))
     return pl.pallas_call(
-        functools.partial(block_kernel, cut),
+        functools.partial(block_kernel, cut, experts),
         out_shape=(
             jax.ShapeDtypeStruct((n, width), bf),
             jax.ShapeDtypeStruct((units, width), f32),
             jax.ShapeDtypeStruct((units, width), f32),
         ),
-        in_specs=[vmem] * 4,
+        in_specs=[vmem] * 5,
         out_specs=(vmem,) * 3,
         scratch_shapes=[
             pltpu.VMEM((NY, NX, n, width), bf),
@@ -381,33 +431,26 @@
             pltpu.VMEM((units, NY * NX * n), f32),
             pltpu.VMEM((units, NY * NX * n), bf),
             pltpu.VMEM((units, NY * NX * n), bf),
-            dma(2),
+            pltpu.VMEM((3, experts, n // experts, width), bf),
+            pltpu.VMEM((3, experts, n // experts, width), bf),
+            pltpu.VMEM((experts, PAD, width), f32),
+            dma(3),
+            pltpu.SemaphoreType.DMA((3, experts)),
+            pltpu.SemaphoreType.DMA((3, experts)),
         ]
         + [dma(SEMS)] * 6,
         compiler_params=pltpu.CompilerParams(
             collective_id=0, has_side_effects=True, vmem_limit_bytes=58 * 1024 * 1024
         ),
-    )(rows, grads, up, down)
+    )(table, rows, grads, up, down)
 
 
 def local(features, classes, live_counts, cotangent, up_weight, down_weight):
     expert_count = lax.axis_size("expert")
-    row_count, width = features.shape
-    span = row_count // expert_count
-    own_table = slot_table(classes, live_counts[0], span, expert_count)
-    both = jnp.concatenate([features, cotangent], axis=1)
-    send = jnp.dot(own_table, both, preferred_element_type=jnp.float32).astype(jnp.bfloat16)
-    send = send.reshape(expert_count, span, 2 * width)
-    came = lax.all_to_all(send, "expert", split_axis=0, concat_axis=0, tiled=True)
-    came = came.reshape(row_count, 2 * width)
-    mine, grad_up, grad_down = block(
-        came[:, :width], came[:, width:], up_weight[0], down_weight[0]
+    table = slot_table(classes, live_counts[0], expert_count)
+    mixed, grad_up, grad_down = block(
+        table, features, cotangent, up_weight[0], down_weight[0], expert_count
     )
-    back = mine.reshape(expert_count, span, width)
-    back = lax.all_to_all(back, "expert", split_axis=0, concat_axis=0, tiled=True)
-    mixed = jnp.dot(
-        own_table.T, back.reshape(row_count, width), preferred_element_type=jnp.float32
-    ).astype(jnp.bfloat16)
     return (mixed, grad_up[None], grad_down[None])
 
 

time: 129 us -> 114 us (0.88)
  Pallas kernels: 77.2 us -> 105 us
  blocking collectives: 21.8 us -> 0 us
  starting transfers between devices: 10.6 us -> 0 us
  waiting for transfers between devices: 8.49 us -> 0 us
  matrix products: 1.99 us -> 0 us
    pallas_call x1, Pallas kernels: 77.2 us -> 105 us  [block(): pl.pallas_call(functools.partial(block_kernel, cut, experts), out_shape=(...]
    all_to_all x1 -> x0, blocking collectives: 21.8 us -> none  [local(): lax.all_to_all(send, 'expert', split_axis=0, concat_axis=0, tiled=True)]
    all_to_all x1 -> x0, starting transfers between devices: 10.6 us -> none  [local(): lax.all_to_all(back, 'expert', split_axis=0, concat_axis=0, tiled=True)]
    all_to_all x1 -> x0, waiting for transfers between devices: 8.49 us -> none  [local(): lax.all_to_all(back, 'expert', split_axis=0, concat_axis=0, tiled=True)]
    dot_general x2 -> x0, matrix products: 1.99 us -> none  [the longest x1 1.12 us: local(): jnp.dot(own_table, both, preferred_element_type=jnp.float32)]
    reshape x4 -> x0, local copies, waits for them, and re-layouts: 1.76 us -> none  [the longest x1 1.57 us: local(): back = mine.reshape(expert_count, span, width)]
    unnamed x4 -> x5, local copies, waits for them, and re-layouts: 3.47 us -> 5.01 us
  transfers between devices with their start and end apart: 1 -> 0, of which waited for: 1 -> 0; matrix products, arithmetic and copies ran while one was open for 0% -> 0% of each run, Pallas kernels for 0% -> 0%
where the time goes in v2:
time: 114 us
  Pallas kernels  105 us (92%)
  local copies, waits for them, and re-layouts  5.01 us (4%)
  other arithmetic  2.21 us (2%)
  between operations  1.29 us (1%)
    pallas_call x1, Pallas kernels, block(): pl.pallas_call(functools.partial(block_kernel, cut, experts), out_shape=(...  105 us
    unnamed x5, local copies, waits for them, and re-layouts  5.01 us

profile of v2, /device:TPU:1, one launch (start us, length us, event | category | flops | bytes accessed | tf_op | source)
XLA Modules:
  0.0 113.9 jit_solution(14036611898438313521)
XLA Ops:
  1.3 0.9 convert_reduce_fusion
  2.2 0.7 multiply_add_fusion
  2.9 0.6 fusion.1.table_ref
  3.5 105.4 %shard_map.85 = (bf16[32,1536]{1,0:T(8,128)(2,1)}, f32[192,1536]{1,0:T(8,128)}, f32[192,1536]{1,0:T(8,128)}) custom-call(bf16[128,32]{1,0:T(8,128)(2,1)} %fusion.1.table_ref, bf16[32,1536]{1,0:T(8,128)(2,1)} %x_ref.1, bf16[32,1536]{1,0:T(8,128)(2,1)} %g_ref.1, bf16[192,1536]{1,0:T(8,128)(2,1)} %bitcast.8, bf16[192,1536]{1,0:T(8,128)(2,1)} %bitcast.9), custom_call_target="tpu_custom_call" | custom-call | tf_op jit(solution)/shard_map/pallas_call | solution.py:414
  108.9 1.5 %copy.13 = bf16[32,1536]{1,0:T(8,128)(2,1)} copy(bf16[32,1536]{1,0:T(8,128)(2,1)} %get-tuple-element.12) | data formatting | bytes 196608
  110.4 0.0 copy-start
  110.4 2.5 %copy.14 = f32[1,192,1536]{2,1,0:T(8,128)} copy(f32[1,192,1536]{2,1,0:T(8,128)} %bitcast.7) | data formatting | bytes 2359296
  112.9 0.0 copy-done
  112.9 1.0 copy.15
  (1 shorter events, 0.0 us)
Async XLA Ops:
  110.4 2.5 %copy-start = (f32[192,1536]{1,0:T(8,128)S(1)}, f32[192,1536]{1,0:T(8,128)}, u32[]{:S(2)}) copy-start(f32[192,1536]{1,0:T(8,128)} %get-tuple-element.8) | copy-start | bytes 3538948

commit v3 on v2

--- a/solution.py
+++ b/solution.py
@@ -9,7 +9,7 @@
 
 NY, NX = 8, 4
 MESH = pl.DeviceIdType.MESH
-SEMS = 52
+SEMS = 76
 PAD = 8
 ROOT = 0.7978845608028654
 CUBE = 0.044715
@@ -188,10 +188,21 @@
     def row_of(offset):
         return lax.rem(y + offset + NY, NY)
 
-    def gather_rounds(t, send_sem, recv_sem):
+    across = (0, 1, -1, 2)
+
+    def column_of(offset):
+        return lax.rem(x + offset + NX, NX)
+
+    def gather_rounds(t, send_sem, recv_sem, ready):
         take, sems = counter(), (send_sem, recv_sem)
         a1 = Spread(NX, x, lambda i, r: t.at[y, i, r, lo], xr, xl, sems, take, sent)
-        a2 = Spread(NY, y, lambda i, r: t.at[i, :, r, lo], yr, yl, sems, take, sent)
+        a2 = {
+            o: Spread(
+                NY, y, (lambda xx: lambda i, r: t.at[i, xx, r, lo])(column_of(o)),
+                yr, yl, sems, take, sent,
+            )
+            for o in across
+        }
         b1 = Spread(NY, y, lambda i, r: t.at[i, x, r, hi], yr, yl, sems, take, sent)
         b2 = {
             o: Spread(
@@ -206,55 +217,80 @@
                 b2[o].wait(1)
                 b2[o].start(2)
 
+        def relay(step, *offs):
+            for o in offs:
+                a2[o].wait(step)
+                a2[o].start(step + 1)
+
+        def whole(*offs):
+            for o in offs:
+                b2[o].wait(2)
+                ready(o)
+
         a1.start(1)
         b1.start(1)
+        a2[0].start(1)
         b2[0].start(1)
         yield
         b1.wait(1)
         b1.start(2)
         a1.wait(1)
         a1.start(2)
-        b2[1].start(1)
-        b2[-1].start(1)
+        for o in (1, -1):
+            a2[o].start(1)
+            b2[o].start(1)
         yield
         b1.wait(2)
         b1.start(3)
-        a1.wait(2)
-        a2.start(1)
         b2[2].start(1)
         b2[-2].start(1)
+        relay(1, 0)
+        a1.wait(2)
+        a2[2].start(1)
         turn(0)
         yield
         b1.wait(3)
         b1.start(4)
         b2[3].start(1)
         b2[-3].start(1)
+        relay(1, 1, -1)
         turn(1, -1)
         yield
         b1.wait(4)
         b2[4].start(1)
-        a2.wait(1)
-        a2.start(2)
+        relay(2, 0)
+        relay(1, 2)
         turn(2, -2)
         yield
-        a2.wait(2)
-        a2.start(3)
+        relay(2, 1, -1)
         turn(3, -3)
-        yield
-        a2.wait(3)
-        a2.start(4)
+        relay(3, 0)
+        relay(2, 2)
+        whole(0)
+        yield
+        relay(3, 1, -1)
         turn(4)
-        yield
-        for o in offsets:
-            b2[o].wait(2)
-        a2.wait(4)
+        relay(3, 2)
+        whole(1, -1)
+        yield
+        whole(2, -2)
+        yield
+        whole(3, -3)
+        yield
+        for o in across:
+            a2[o].wait(4)
+        whole(4)
 
     def sum_rounds():
         take, sems = counter(), (rsend, rrecv)
-        a2 = Gather(
-            NY, y, lambda i, r: part.at[i, :, r, lo], yr, yl, sems, take, sent,
-            slot=lambda w, s, r: ra2.at[w, s, :, r, :],
-        )
+        a2 = {
+            o: Gather(
+                NY, y, (lambda xx: lambda i, r: part.at[i, xx, r, lo])(column_of(o)),
+                yr, yl, sems, take, sent,
+                slot=(lambda m: lambda w, s, r: ra2.at[m, w, s, r, :])(m),
+            )
+            for m, o in enumerate(across)
+        }
         a1 = Gather(
             NX, x, lambda i, r: part.at[y, i, r, lo], xr, xl, sems, take, sent,
             slot=lambda w, s, r: ra1.at[w, s, r, :],
@@ -267,9 +303,9 @@
             o: Gather(
                 NX, x, (lambda yy: lambda i, r: part.at[yy, i, r, hi])(row_of(o)),
                 xr, xl, sems, take, sent,
-                slot=(lambda n: lambda w, s, r: rb2.at[n, w, s, r, :])(n),
+                slot=(lambda m: lambda w, s, r: rb2.at[m, w, s, r, :])(m),
             )
-            for n, o in enumerate(offsets)
+            for m, o in enumerate(offsets)
         }
 
         def turn(*offs):
@@ -277,48 +313,62 @@
                 b2[o].add(1)
                 b2[o].start(2)
 
+        def relay(step, *offs):
+            for o in offs:
+                a2[o].add(step)
+                a2[o].start(step + 1)
+
         def done(*offs):
             for o in offs:
                 b2[o].add(2)
 
-        a2.start(1)
-        for o in (4, 3, -3, 2, -2):
-            b2[o].start(1)
+        b2[4].start(1)
+        a2[2].start(1)
+        for o in (1, -1):
+            a2[o].start(1)
+            b2[3 * o].start(1)
+        a2[0].start(1)
+        b2[2].start(1)
+        b2[-2].start(1)
         yield
         turn(4)
-        a2.add(1)
-        a2.start(2)
+        relay(1, 2)
         turn(3, -3)
+        relay(1, 1, -1, 0)
         for o in (1, -1, 0):
             b2[o].start(1)
         yield
         done(4)
         b1.start(1)
+        relay(2, 2)
         turn(2, -2)
-        yield
-        a2.add(2)
-        a2.start(3)
+        relay(2, 1, -1)
+        yield
         done(3, -3)
         b1.add(1)
         b1.start(2)
+        relay(2, 0)
+        relay(3, 2)
         turn(1, -1, 0)
         yield
-        a2.add(3)
-        a2.start(4)
+        relay(3, 1, -1)
         done(2, -2)
         b1.add(2)
         b1.start(3)
-        yield
-        a2.add(4)
+        relay(3, 0)
+        a2[2].add(4)
         a1.start(1)
+        yield
         done(1, -1)
         b1.add(3)
         b1.start(4)
-        yield
+        a2[1].add(4)
+        a2[-1].add(4)
         a1.add(1)
         a1.start(2)
+        yield
+        a2[0].add(4)
         done(0)
-        yield
         b1.add(4)
         a1.add(2)
 
@@ -326,32 +376,26 @@
     tn = (((0,), (0,)), ((), ()))
     chunk = NX * 32
 
-    def forward(first, last):
-        def body(c, carry):
-            rows = xs[c].reshape(chunk, width)
-            v = lax.dot_general(up_ref[...], rows, nt, preferred_element_type=jnp.float32)
-            t = jnp.tanh(ROOT * (v + CUBE * v * v * v))
-            columns = pl.ds(pl.multiple_of(c * chunk, chunk), chunk)
-            slope_of[:, columns] = 0.5 * (1.0 + t) + 0.5 * v * (1.0 - t * t) * (
-                ROOT * (1.0 + 3.0 * CUBE * v * v)
-            )
-            h = (0.5 * v * (1.0 + t)).astype(jnp.bfloat16)
-            hid[:, columns] = h
-            p = lax.dot_general(h, down_ref[...], tn, preferred_element_type=jnp.float32)
-            part[c] = p.astype(jnp.bfloat16).reshape(NX, 32, width)
-            return carry
-
-        lax.fori_loop(first, last, body, 0)
-
-    def backward():
-        def body(c, carry):
-            rows = gs[c].reshape(chunk, width)
-            v = lax.dot_general(down_ref[...], rows, nt, preferred_element_type=jnp.float32)
-            columns = pl.ds(pl.multiple_of(c * chunk, chunk), chunk)
-            igr[:, columns] = (v * slope_of[:, columns]).astype(jnp.bfloat16)
-            return carry
-
-        lax.fori_loop(0, NY, body, 0)
+    def forward(offset):
+        c = row_of(offset)
+        rows = xs[c].reshape(chunk, width)
+        v = lax.dot_general(up_ref[...], rows, nt, preferred_element_type=jnp.float32)
+        t = jnp.tanh(ROOT * (v + CUBE * v * v * v))
+        columns = pl.ds(pl.multiple_of(c * chunk, chunk), chunk)
+        slope_of[:, columns] = 0.5 * (1.0 + t) + 0.5 * v * (1.0 - t * t) * (
+            ROOT * (1.0 + 3.0 * CUBE * v * v)
+        )
+        h = (0.5 * v * (1.0 + t)).astype(jnp.bfloat16)
+        hid[:, columns] = h
+        p = lax.dot_general(h, down_ref[...], tn, preferred_element_type=jnp.float32)
+        part[c] = p.astype(jnp.bfloat16).reshape(NX, 32, width)
+
+    def backward(offset):
+        c = row_of(offset)
+        rows = gs[c].reshape(chunk, width)
+        v = lax.dot_general(down_ref[...], rows, nt, preferred_element_type=jnp.float32)
+        columns = pl.ds(pl.multiple_of(c * chunk, chunk), chunk)
+        igr[:, columns] = (v * slope_of[:, columns]).astype(jnp.bfloat16)
 
     def weight_sums(left, t, out):
         tile = min(256, width)
@@ -364,38 +408,26 @@
 
         lax.fori_loop(0, width // tile, body, 0)
 
-    xg = gather_rounds(xs, xsend, xrecv)
-    gg = gather_rounds(gs, gsend, grecv)
-    for _ in range(2):
+    xg = gather_rounds(xs, xsend, xrecv, forward)
+    gg = gather_rounds(gs, gsend, grecv, backward)
+    rg = sum_rounds()
+    for _ in range(3):
         next(xg)
     gs[y, x] = arrive(1, dense)
     for _ in range(2):
         next(xg)
-    next(gg)
-    next(xg)
-    next(gg)
-    next(xg)
-    next(gg)
-    next(xg)
+    for _ in range(4):
+        next(gg)
+        next(xg)
     next(gg)
     next(xg, None)
-    forward(0, NY // 2)
-    next(gg)
-    forward(NY // 2, NY)
-    rg = sum_rounds()
-    next(rg)
-    next(gg)
-    next(rg)
-    next(gg)
-    next(rg)
-    next(gg, None)
-    backward()
-    next(rg)
+    for _ in range(5):
+        next(rg)
+        next(gg, None)
     weight_sums(hid, gs, gdown_ref)
     next(rg)
     weight_sums(igr, xs, gup_ref)
-    for _ in rg:
-        pass
+    next(rg, None)
     fill(2, dense, part[y, x])
     leave(2)
     mixed_ref[...] = arrive(2, table_ref[...])
@@ -424,7 +456,7 @@
             pltpu.VMEM((NY, NX, n, width), bf),
             pltpu.VMEM((NY, NX, n, width), bf),
             pltpu.VMEM((NY, NX, n, width), bf),
-            pltpu.VMEM((2, 4, NX, n, cut), bf),
+            pltpu.VMEM((NX, 2, 4, n, cut), bf),
             pltpu.VMEM((2, 2, n, cut), bf),
             pltpu.VMEM((8, 2, 2, n, rest), bf),
             pltpu.VMEM((2, 4, n, rest), bf),

time: 114 us -> 105 us (0.921)
  Pallas kernels: 105 us -> 96.2 us
    pallas_call x1, Pallas kernels: 105 us -> 96.2 us  [block(): pl.pallas_call(functools.partial(block_kernel, cut, experts), out_shape=(...]
where the time goes in v3:
time: 105 us
  Pallas kernels  96.2 us (92%)
  local copies, waits for them, and re-layouts  5.01 us (5%)
  other arithmetic  2.21 us (2%)
  between operations  1.29 us (1%)
    pallas_call x1, Pallas kernels, block(): pl.pallas_call(functools.partial(block_kernel, cut, experts), out_shape=(...  96.2 us
    unnamed x5, local copies, waits for them, and re-layouts  5.01 us

profile of v3, /device:TPU:1, one launch (start us, length us, event | category | flops | bytes accessed | tf_op | source)
XLA Modules:
  0.0 104.7 jit_solution(8064240392057743899)
XLA Ops:
  1.3 0.9 convert_reduce_fusion
  2.2 0.7 multiply_add_fusion
  2.9 0.6 fusion.1.table_ref
  3.5 96.2 %shard_map.85 = (bf16[32,1536]{1,0:T(8,128)(2,1)}, f32[192,1536]{1,0:T(8,128)}, f32[192,1536]{1,0:T(8,128)}) custom-call(bf16[128,32]{1,0:T(8,128)(2,1)} %fusion.1.table_ref, bf16[32,1536]{1,0:T(8,128)(2,1)} %x_ref.1, bf16[32,1536]{1,0:T(8,128)(2,1)} %g_ref.1, bf16[192,1536]{1,0:T(8,128)(2,1)} %bitcast.8, bf16[192,1536]{1,0:T(8,128)(2,1)} %bitcast.9), custom_call_target="tpu_custom_call" | custom-call | tf_op jit(solution)/shard_map/pallas_call | solution.py:446
  99.7 1.5 %copy.13 = bf16[32,1536]{1,0:T(8,128)(2,1)} copy(bf16[32,1536]{1,0:T(8,128)(2,1)} %get-tuple-element.12) | data formatting | bytes 196608
  101.3 0.0 copy-start
  101.3 2.5 %copy.14 = f32[1,192,1536]{2,1,0:T(8,128)} copy(f32[1,192,1536]{2,1,0:T(8,128)} %bitcast.7) | data formatting | bytes 2359296
  103.7 0.0 copy-done
  103.7 1.0 copy.15
  (1 shorter events, 0.0 us)
Async XLA Ops:
  101.3 2.5 %copy-start = (f32[192,1536]{1,0:T(8,128)S(1)}, f32[192,1536]{1,0:T(8,128)}, u32[]{:S(2)}) copy-start(f32[192,1536]{1,0:T(8,128)} %get-tuple-element.8) | copy-start | bytes 3538948

commit v4 on v3

--- a/solution.py
+++ b/solution.py
@@ -15,18 +15,18 @@
 CUBE = 0.044715
 
 
-def slot_table(group_classes, group_counts, expert_count):
-    row_count = group_classes.shape[0]
-    position = lax.broadcasted_iota(jnp.int32, (1, row_count), 1)
-    live = position < group_counts
-    same = group_classes[:, None] == group_classes[None, :]
-    later = lax.broadcasted_iota(jnp.int32, (row_count, row_count), 0)
-    sooner = lax.broadcasted_iota(jnp.int32, (row_count, row_count), 1)
-    place = jnp.sum((same & (sooner < later)).astype(jnp.int32), axis=1)
-    target = group_classes * PAD + place
-    slots = lax.broadcasted_iota(jnp.int32, (expert_count * PAD, 1), 0)
-    chosen = (target[None, :] == slots) & live
-    return chosen.astype(jnp.bfloat16)
+def slot_table(labels, live, experts):
+    count = labels.shape[1]
+    across = jnp.broadcast_to(labels, (count, count)).astype(jnp.float32)
+    down = across.T
+    sooner = lax.broadcasted_iota(jnp.int32, (count, count), 0)
+    later = lax.broadcasted_iota(jnp.int32, (count, count), 1)
+    earlier = jnp.where((across == down) & (sooner < later), 1.0, 0.0)
+    place = jnp.sum(earlier, axis=0, keepdims=True).astype(jnp.int32)
+    position = lax.broadcasted_iota(jnp.int32, (1, count), 1)
+    target = jnp.where(position < live, labels * PAD + place, -1)
+    slots = lax.broadcasted_iota(jnp.int32, (experts * PAD, count), 0)
+    return jnp.where(slots == target, 1.0, 0.0).astype(jnp.bfloat16)
 
 
 class Line:
@@ -108,7 +108,7 @@
 
 
 def block_kernel(
-    cut, experts, table_ref, x_ref, g_ref, up_ref, down_ref, mixed_ref, gup_ref, gdown_ref,
+    cut, experts, class_ref, live_ref, x_ref, g_ref, up_ref, down_ref, mixed_ref, gup_ref, gdown_ref,
     xs, gs, part, ra2, ra1, rb2, rb1, slope_of, hid, igr, out_to, in_from, wide,
     own_sem, dsend, drecv, xsend, xrecv, gsend, grecv, rsend, rrecv,
 ):
@@ -176,10 +176,11 @@
     row = lax.broadcasted_iota(jnp.int32, (experts * PAD, n), 1)
     dense = (slot == lax.div(row, span) * PAD + lax.rem(row, span)).astype(jnp.bfloat16)
     sent = []
-    fill(0, table_ref[...], x_ref[...])
+    table = slot_table(class_ref[...], live_ref[...], experts)
+    fill(0, table, x_ref[...])
     pl.semaphore_wait(barrier, 3 + experts)
     leave(0)
-    fill(1, table_ref[...], g_ref[...])
+    fill(1, table, g_ref[...])
     leave(1)
     xs[y, x] = arrive(0, dense)
 
@@ -424,18 +425,18 @@
     for _ in range(5):
         next(rg)
         next(gg, None)
-    weight_sums(hid, gs, gdown_ref)
-    next(rg)
-    weight_sums(igr, xs, gup_ref)
-    next(rg, None)
+    for _ in rg:
+        pass
     fill(2, dense, part[y, x])
     leave(2)
-    mixed_ref[...] = arrive(2, table_ref[...])
+    weight_sums(hid, gs, gdown_ref)
+    weight_sums(igr, xs, gup_ref)
+    mixed_ref[...] = arrive(2, table)
     for copy in sent:
         copy.wait_send()
 
 
-def block(table, rows, grads, up, down, experts):
+def block(labels, live, rows, grads, up, down, experts):
     n, width = rows.shape
     units = up.shape[0]
     cut = max(1, (width // 128) * 5 // 12) * 128
@@ -450,7 +451,7 @@
             jax.ShapeDtypeStruct((units, width), f32),
             jax.ShapeDtypeStruct((units, width), f32),
         ),
-        in_specs=[vmem] * 5,
+        in_specs=[vmem] * 6,
         out_specs=(vmem,) * 3,
         scratch_shapes=[
             pltpu.VMEM((NY, NX, n, width), bf),
@@ -474,14 +475,14 @@
         compiler_params=pltpu.CompilerParams(
             collective_id=0, has_side_effects=True, vmem_limit_bytes=58 * 1024 * 1024
         ),
-    )(table, rows, grads, up, down)
+    )(labels, live, rows, grads, up, down)
 
 
 def local(features, classes, live_counts, cotangent, up_weight, down_weight):
     expert_count = lax.axis_size("expert")
-    table = slot_table(classes, live_counts[0], expert_count)
     mixed, grad_up, grad_down = block(
-        table, features, cotangent, up_weight[0], down_weight[0], expert_count
+        classes[None, :], live_counts[None, :], features, cotangent,
+        up_weight[0], down_weight[0], expert_count,
     )
     return (mixed, grad_up[None], grad_down[None])
 

time: 105 us -> 103 us (0.981)
  other arithmetic: 2.21 us -> 0 us
where the time goes in v4:
time: 103 us
  Pallas kernels  96.2 us (93%)
  local copies, waits for them, and re-layouts  5.01 us (5%)
  between operations  1.29 us (1%)
    pallas_call x1, Pallas kernels, block(): pl.pallas_call(functools.partial(block_kernel, cut, experts), out_shape=(...  96.2 us
    unnamed x5, local copies, waits for them, and re-layouts  5.01 us

profile of v4, /device:TPU:1, one launch (start us, length us, event | category | flops | bytes accessed | tf_op | source)
XLA Modules:
  0.0 102.5 jit_solution(12465082823351442908)
XLA Ops:
  1.3 96.2 %shard_map.85 = (bf16[32,1536]{1,0:T(8,128)(2,1)}, f32[192,1536]{1,0:T(8,128)}, f32[192,1536]{1,0:T(8,128)}) custom-call(s32[1,32]{1,0:T(1,128)} %bitcast.11, s32[1,1]{1,0:T(1,128)} %bitcast.6.live_ref, bf16[32,1536]{1,0:T(8,128)(2,1)} %x_ref.1, bf16[32,1536]{1,0:T(8,128)(2,1)} %g_ref.1, bf16[192,1536]{1,0:T(8,128)(2,1)} %bitcast.9, bf16[192,1536]{1,0:T(8,128)(2,1)} %bitcast.10), custom_call_target="tpu_custom_call" | custom-call | tf_op jit(solution)/shard_map/pallas_call | solution.py:447
  97.5 1.5 %copy.13 = bf16[32,1536]{1,0:T(8,128)(2,1)} copy(bf16[32,1536]{1,0:T(8,128)(2,1)} %get-tuple-element.12) | data formatting | bytes 196608
  99.0 0.0 copy-start
  99.0 2.5 %copy.14 = f32[1,192,1536]{2,1,0:T(8,128)} copy(f32[1,192,1536]{2,1,0:T(8,128)} %bitcast.8) | data formatting | bytes 2359296
  101.5 0.0 copy-done
  101.5 1.0 copy.15
Async XLA Ops:
  99.0 2.5 %copy-start = (f32[192,1536]{1,0:T(8,128)S(1)}, f32[192,1536]{1,0:T(8,128)}, u32[]{:S(2)}) copy-start(f32[192,1536]{1,0:T(8,128)} %get-tuple-element.8) | copy-start | bytes 3538948

commit v5 on v4

--- a/solution.py
+++ b/solution.py
@@ -148,7 +148,7 @@
     def own(k):
         return pltpu.make_async_copy(out_to.at[k, e], in_from.at[k, e], own_sem.at[k])
 
-    near = [d for h in range(1, experts // 2 + 1) for d in sorted({h, experts - h})]
+    far_first = [d for h in range(experts // 2, 0, -1) for d in sorted({h, experts - h})]
 
     def fill(k, table, rows):
         spread = jnp.dot(table, rows, preferred_element_type=jnp.float32)
@@ -156,14 +156,14 @@
 
     def leave(k):
         own(k).start()
-        for d in near:
+        for d in far_first:
             copy = exchange(k, d, 1)
             copy.start()
             sent.append(copy)
 
     def arrive(k, table):
         own(k).wait()
-        for d in near:
+        for d in far_first:
             exchange(k, d, -1).wait_recv()
         wide[:, :span, :] = in_from[k].astype(jnp.float32)
         flat = wide[...].reshape(experts * PAD, width).astype(jnp.bfloat16)
@@ -180,8 +180,6 @@
     fill(0, table, x_ref[...])
     pl.semaphore_wait(barrier, 3 + experts)
     leave(0)
-    fill(1, table, g_ref[...])
-    leave(1)
     xs[y, x] = arrive(0, dense)
 
     offsets = (0, 1, -1, 2, -2, 3, -3, 4)
@@ -412,11 +410,12 @@
     xg = gather_rounds(xs, xsend, xrecv, forward)
     gg = gather_rounds(gs, gsend, grecv, backward)
     rg = sum_rounds()
-    for _ in range(3):
+    next(xg)
+    fill(1, table, g_ref[...])
+    leave(1)
+    for _ in range(4):
         next(xg)
     gs[y, x] = arrive(1, dense)
-    for _ in range(2):
-        next(xg)
     for _ in range(4):
         next(gg)
         next(xg)

time: 103 us -> 101 us (0.981)
  Pallas kernels: 96.2 us -> 95 us
    pallas_call x1, Pallas kernels: 96.2 us -> 95 us  [block(): pl.pallas_call(functools.partial(block_kernel, cut, experts), out_shape=(...]
where the time goes in v5:
time: 101 us
  Pallas kernels  95 us (94%)
  local copies, waits for them, and re-layouts  5.01 us (5%)
  between operations  1.29 us (1%)
    pallas_call x1, Pallas kernels, block(): pl.pallas_call(functools.partial(block_kernel, cut, experts), out_shape=(...  95 us
    unnamed x5, local copies, waits for them, and re-layouts  5.01 us

profile of v5, /device:TPU:1, one launch (start us, length us, event | category | flops | bytes accessed | tf_op | source)
XLA Modules:
  0.0 101.3 jit_solution(12922472165589287053)
XLA Ops:
  1.3 95.0 %shard_map.85 = (bf16[32,1536]{1,0:T(8,128)(2,1)}, f32[192,1536]{1,0:T(8,128)}, f32[192,1536]{1,0:T(8,128)}) custom-call(s32[1,32]{1,0:T(1,128)} %bitcast.11, s32[1,1]{1,0:T(1,128)} %bitcast.6.live_ref, bf16[32,1536]{1,0:T(8,128)(2,1)} %x_ref.1, bf16[32,1536]{1,0:T(8,128)(2,1)} %g_ref.1, bf16[192,1536]{1,0:T(8,128)(2,1)} %bitcast.9, bf16[192,1536]{1,0:T(8,128)(2,1)} %bitcast.10), custom_call_target="tpu_custom_call" | custom-call | tf_op jit(solution)/shard_map/pallas_call | solution.py:446
  96.3 1.5 %copy.13 = bf16[32,1536]{1,0:T(8,128)(2,1)} copy(bf16[32,1536]{1,0:T(8,128)(2,1)} %get-tuple-element.12) | data formatting | bytes 196608
  97.8 0.0 copy-start
  97.8 2.5 %copy.14 = f32[1,192,1536]{2,1,0:T(8,128)} copy(f32[1,192,1536]{2,1,0:T(8,128)} %bitcast.8) | data formatting | bytes 2359296
  100.3 0.0 copy-done
  100.3 1.0 %copy.15 = f32[1,192,1536]{2,1,0:T(8,128)} copy(f32[1,192,1536]{2,1,0:T(8,128)S(1)} %bitcast.7) | data formatting | bytes 2359296
Async XLA Ops:
  97.8 2.5 %copy-start = (f32[192,1536]{1,0:T(8,128)S(1)}, f32[192,1536]{1,0:T(8,128)}, u32[]{:S(2)}) copy-start(f32[192,1536]{1,0:T(8,128)} %get-tuple-element.8) | copy-start | bytes 3538948
